TPU v7x, 256 devices: a whole 4x4x8 slice. The times are simulated.
256 devices in a mesh: mic: 4 (over y), seq: 64 (over z, x, core).
Axes of the slice: x: 4, y: 4, z: 8, core: 2. Of those that a mesh axis runs over, the one named last changes fastest.
Arguments:
- frames_in: bfloat16 [8, 32768, 512], P('mic', 'seq'), may hold values from -16 to 16
- w_qkv: bfloat16 [8, 512, 1536], P('mic'), may hold values from -0.25 to 0.25
- w_join: bfloat16 [4096, 1024], P(('mic', 'seq')), may hold values from -0.09375 to 0.09375
- norm_gain: float32 [1024], replicated, may hold values from 0.5 to 2
- w_router: bfloat16 [1024, 64], replicated, may hold values from -0.1875 to 0.1875
- w_gate: bfloat16 [64, 1024, 4096], P('seq', None, 'mic'), may hold values from -0.1875 to 0.1875
- w_up: bfloat16 [64, 1024, 4096], P('seq', None, 'mic'), may hold values from -0.1875 to 0.1875
- w_down: bfloat16 [64, 4096, 1024], P('seq', 'mic'), may hold values from -0.09375 to 0.09375
- expert_ids: int32 [64, 4, 128, 2], P('seq', 'mic'), may hold values from 0 to 63, all different within a row; in each aligned block of 128 rows (0 to 127, 128 to 255, ..., all dimensions but the last counted through in order) at most 6 rows name the same one
Outputs:
- layer_out: bfloat16 [64, 4, 128, 1024], P('seq', 'mic')
Inputs may be any that keep to these rules, and one draw needn't show every extreme that they name: `expert_ids`: in the rows of one block (128 frames) no expert is named more than 6 times, a bound that some block reaches; the two ids of a frame differ.
All inputs are finite; a program needn't handle non-finite values.
Results may differ from a plain program's by a relative error of at most 0.017.
Values may be sent and summed in bfloat16 or wider, within the bound.
A program may use at most 128 MiB of HBM per device.

v0:
```python
import jax
import jax.numpy as jnp
from jax import lax
from jax.sharding import PartitionSpec as P

MICS = 8
HEADS = 8
TOP = 2


def body(frames_in, w_qkv, w_join, norm_gain, w_router, w_gate, w_up, w_down, expert_ids):
    mic_count = lax.axis_size("mic")
    seq_count = lax.axis_size("seq")
    mic_local, span, chan_width = frames_in.shape
    frame_rows = span // mic_count
    head_dim = chan_width // HEADS
    model_width = w_join.shape[1]
    expert_count = w_router.shape[1]
    exp_local = w_gate.shape[0]
    capacity = max(2, 3 * TOP * frame_rows // (2 * expert_count))
    projected = jnp.einsum(
        "mfc,mce->mfe", frames_in, w_qkv, preferred_element_type=jnp.float32
    ).astype(jnp.bfloat16)
    projected = projected.reshape(mic_local, mic_count, frame_rows, 3 * chan_width)
    arrived_block = lax.all_to_all(projected, "mic", split_axis=1, concat_axis=0, tiled=True)
    arrived_block = arrived_block[:, 0]
    frame_count = arrived_block.shape[1]
    queries = arrived_block[..., :chan_width].reshape(MICS, frame_count, HEADS, head_dim)
    keys_all = arrived_block[..., chan_width : 2 * chan_width].reshape(
        MICS, frame_count, HEADS, head_dim
    )
    values_all = arrived_block[..., 2 * chan_width :].reshape(MICS, frame_count, HEADS, head_dim)
    scores = jnp.einsum(
        "ifhd,jfhd->fhij", queries, keys_all, preferred_element_type=jnp.float32
    ) * head_dim ** (-0.5)
    row_max = jnp.max(scores, axis=-1, keepdims=True)
    weights = jnp.exp(scores - row_max)
    probs = (weights / jnp.sum(weights, axis=-1, keepdims=True)).astype(jnp.bfloat16)
    mixed_heads = jnp.einsum(
        "fhij,jfhd->fihd", probs, values_all, preferred_element_type=jnp.float32
    )
    attended = mixed_heads.astype(jnp.bfloat16).reshape(frame_count, MICS * chan_width)
    joined = jnp.dot(
        attended,
        lax.all_gather(w_join, ("mic", "seq"), axis=0, tiled=True),
        preferred_element_type=jnp.float32,
    )
    scale_row = lax.rsqrt(jnp.mean(joined * joined, axis=-1, keepdims=True) + 1e-06)
    normed = (joined * scale_row * norm_gain).astype(jnp.bfloat16)
    logits = jnp.dot(normed, w_router, preferred_element_type=jnp.float32)
    expert_rows = expert_ids.reshape(frame_rows, TOP)
    chosen = (expert_rows[..., None] == jnp.arange(expert_count, dtype=jnp.int32)).astype(jnp.int32)
    picked = jnp.sum(logits[:, None, :] * chosen.astype(jnp.float32), axis=-1)
    first_gate = 1.0 / (1.0 + jnp.exp(picked[:, 1] - picked[:, 0]))
    gates = jnp.stack([first_gate, 1.0 - first_gate], axis=-1)
    counts = jnp.sum(chosen, axis=1)
    before = jnp.cumsum(counts, axis=0) - counts
    slot_index = jnp.sum(before[:, None, :] * chosen, axis=-1)
    in_slot = slot_index[..., None] == jnp.arange(capacity, dtype=jnp.int32)
    mapped = (
        ((chosen[..., :, None] == 1) & in_slot[..., None, :])
        .reshape(frame_rows, TOP, expert_count * capacity)
        .astype(jnp.bfloat16)
    )
    merged_map = jnp.sum(mapped, axis=1)
    buffers = jnp.einsum(
        "rs,rd->sd", merged_map, normed, preferred_element_type=jnp.float32
    ).astype(jnp.bfloat16)
    buffers = buffers.reshape(seq_count, exp_local * capacity, model_width)
    landed = lax.all_to_all(buffers, "seq", split_axis=0, concat_axis=0, tiled=True)
    arrived = lax.all_gather(landed[None], "mic", axis=0, tiled=True)
    flat = arrived.reshape(mic_count * seq_count * exp_local * capacity, model_width)
    piece_rows = flat.reshape(-1, exp_local, capacity, model_width)
    first_proj = jnp.einsum(
        "nejd,edf->nejf", piece_rows, w_gate, preferred_element_type=jnp.float32
    )
    second_proj = jnp.einsum("nejd,edf->nejf", piece_rows, w_up, preferred_element_type=jnp.float32)
    inner = (jax.nn.silu(first_proj) * second_proj).astype(jnp.bfloat16)
    result = jnp.einsum("nejf,efd->nejd", inner, w_down, preferred_element_type=jnp.float32)
    summed = lax.psum_scatter(
        result.reshape(
            lax.axis_size("mic") * (seq_count * exp_local * capacity), model_width
        ).astype(jnp.bfloat16),
        "mic",
        scatter_dimension=0,
        tiled=True,
    ).astype(jnp.float32)
    summed = summed.astype(jnp.bfloat16).reshape(seq_count, exp_local * capacity, model_width)
    returned = lax.all_to_all(summed, "seq", split_axis=0, concat_axis=0, tiled=True)
    returned = returned.reshape(expert_count * capacity, model_width)
    picked_out = jnp.einsum("rks,sd->rkd", mapped, returned, preferred_element_type=jnp.float32)
    total = joined + jnp.sum(gates[..., None] * picked_out, axis=1)
    return total.astype(jnp.bfloat16).reshape(1, 1, frame_rows, model_width)


def solution(mesh):
    return jax.shard_map(
        body,
        mesh=mesh,
        in_specs=(
            P("mic", "seq", None),
            P("mic", None, None),
            P(("mic", "seq"), None),
            P(),
            P(),
            P("seq", None, "mic"),
            P("seq", None, "mic"),
            P("seq", "mic", None),
            P("seq", "mic", None, None),
        ),
        out_specs=P("seq", "mic", None, None),
        check_vma=False,
    )
```

profile of v0, /device:TPU:1, one launch (start us, length us, event | category | flops | bytes accessed | tf_op | source)
XLA Modules:
  0.0 346.4 jit_solution(7928431488291336185)
XLA Ops:
  8.4 3.0 convolution_convert_fusion
  11.5 2.0 copy.26
  13.4 5.1 %all-to-all-start = ((bf16[2,4,128,1536]{3,2,0,1:T(8,128)(2,1)}), bf16[2,4,128,1536]{3,2,0,1:T(8,128)(2,1)S(1)}, u32[]{:S(2)}, u32[]{:S(2)}) async-start(bf16[2,4,128,1536]{3,2,0,1:T(8,128)(2,1)} %copy.26), calls=%async_computation | async-start | bytes 6291456 | tf_op jit(solution)/shard_map/all_to_all | solution.py:25
  19.2 35.4 %all-to-all-done = bf16[2,4,128,1536]{3,2,0,1:T(8,128)(2,1)S(1)} async-done(((bf16[2,4,128,1536]{3,2,0,1:T(8,128)(2,1)}), bf16[2,4,128,1536]{3,2,0,1:T(8,128)(2,1)S(1)}, u32[]{:S(2)}, u32[]{:S(2)}) %all-to-all-start) | async-done | bytes 3145760 | tf_op jit(solution)/shard_map/all_to_all | solution.py:25
  58.1 3.8 %copy.30 = bf16[8,128,8,64]{3,0,2,1:T(8,128)(2,1)} copy(bf16[8,128,8,64]{1,3,2,0:T(8,128)(2,1)S(1)} %bitcast.103) | data formatting | bytes 2097152 | tf_op jit(solution)/shard_map/reshape | solution.py:28
  62.5 3.7 %copy.31 = bf16[8,128,8,64]{3,0,2,1:T(8,128)(2,1)} copy(bf16[8,128,8,64]{1,3,2,0:T(8,128)(2,1)S(1)} %bitcast.104) | data formatting | bytes 2097152 | tf_op jit(solution)/shard_map/reshape | solution.py:29
  66.9 3.7 %copy.32 = bf16[8,128,8,64]{3,0,2,1:T(8,128)(2,1)} copy(bf16[8,128,8,64]{1,3,2,0:T(8,128)(2,1)S(1)} %bitcast.105) | data formatting | bytes 2097152 | tf_op jit(solution)/shard_map/reshape | solution.py:32
  70.6 6.6 %fusion.38 = (f32[128,8,8]{2,1,0:T(8,128)S(1)}, f32[128,8,8,8]{2,3,1,0:T(8,128)}) fusion(bf16[8,128,8,64]{3,0,2,1:T(8,128)(2,1)S(1)} %copy-done.5, bf16[8,128,8,64]{3,0,2,1:T(8,128)(2,1)} %copy.31), kind=kOutput, calls=%fused_computation.56 | convolution fusion | flops 8585223 | bytes 2392064 | tf_op jit(solution)/shard_map/sub | solution.py:37
  77.2 4.7 %convert_bitcast_fusion.1 = bf16[128,8,8,64]{3,1,2,0:T(8,128)(2,1)} fusion(bf16[8,128,8,64]{3,0,2,1:T(8,128)(2,1)} %copy.32, f32[128,8,8,8]{2,3,1,0:T(8,128)} %get-tuple-element.11, f32[128,8,8]{2,1,0:T(8,128)S(1)} %get-tuple-element.10), kind=kOutput, calls=%fused_computation.22 | convolution fusion | flops 9043968 | bytes 2392064 | tf_op jit(solution)/shard_map/fhij,jfhd->fihd/dot_general | solution.py:39
  81.9 3.2 copy.34
  85.1 59.5 %all-gather.4.cloned.1.call-done = bf16[4096,1024]{1,0:T(8,128)(2,1)} async-done(((bf16[16,1024]{1,0:T(8,128)(2,1)}), bf16[4096,1024]{1,0:T(8,128)(2,1)}) %all-gather.4.cloned.1.call-update) | async-done | bytes 8388624 | tf_op jit(solution)/shard_map/all_gather | solution.py:45
  144.6 4.7 %multiply_reduce_fusion.1 = (f32[128]{0:T(128)S(1)}, f32[128,1024]{1,0:T(8,128)S(1)}) fusion(bf16[128,4096]{0,1:T(8,128)(2,1)S(1)} %bitcast.102, bf16[4096,1024]{1,0:T(8,128)(2,1)} %all-gather.4.cloned.1.call-done), kind=kOutput, calls=%fused_computation.33 | convolution fusion | flops 1074003840 | bytes 9961984 | tf_op jit(solution)/shard_map/dot_general | solution.py:43
  150.0 35.1 %all_to_all.25 = bf16[64,6,1024]{2,1,0:T(8,128)(2,1)S(1)} all-to-all(bf16[64,6,1024]{2,1,0:T(8,128)(2,1)S(1)} %reshape.92), channel_id=1, replica_groups=mesh['mic'=4,'seq'=64] {'seq'}, dimensions={0} | all-to-all | bytes 1572864 | tf_op jit(solution)/shard_map/all_to_all | solution.py:70
  186.5 37.7 %all-gather.6.cloned.1.call-done = bf16[256,6,1024]{2,0,1:T(8,128)(2,1)} async-done(((bf16[64,6,1024]{2,0,1:T(8,128)(2,1)}), bf16[256,6,1024]{2,0,1:T(8,128)(2,1)}) %all-gather.6.cloned.1.call-update) | async-done | bytes 3145744 | tf_op jit(solution)/shard_map/all_gather | solution.py:71
  224.2 8.6 %fusion.19 = f32[256,6,1024]{2,0,1:T(8,128)} fusion(bf16[256,6,1024]{2,0,1:T(8,128)(2,1)} %all-gather.6.cloned.1.call-done, bf16[1,1024,1024]{2,1,0:T(8,128)(2,1)} %param.14), kind=kOutput, calls=%fused_computation.20 | convolution fusion | flops 3221225472 | bytes 11534336 | tf_op jit(solution)/shard_map/nejd,edf->nejf/dot_general | solution.py:74
  232.8 10.6 %convert_bitcast_fusion = bf16[256,1,6,1024]{3,0,2,1:T(8,128)(2,1)S(1)} fusion(f32[256,6,1024]{2,0,1:T(8,128)} %fusion.19, bf16[256,6,1024]{2,0,1:T(8,128)(2,1)} %all-gather.6.cloned.1.call-done, bf16[1,1024,1024]{2,1,0:T(8,128)(2,1)} %param.16, bf16[1,1024,1024]{2,1,0:T(8,128)(2,1)} %param.15), kind=kOutput, calls=%fused_computation.15 | convolution fusion | flops 6453460992 | bytes 16777216 | tf_op jit(solution)/shard_map/nejf,efd->nejd/dot_general | solution.py:79
  243.4 3.7 %copy.40 = bf16[256,1,6,1024]{3,2,0,1:T(8,128)(2,1)} copy(bf16[256,1,6,1024]{3,0,2,1:T(8,128)(2,1)S(1)} %convert_bitcast_fusion) | data formatting | bytes 6291456 | tf_op jit(solution)/shard_map/convert_element_type | solution.py:83
  247.1 6.3 %convert_element_type.71 = bf16[1536,1024]{1,0:T(8,128)(2,1)} reshape(bf16[256,1,6,1024]{3,2,0,1:T(8,128)(2,1)} %copy.40) | data formatting | bytes 6291456 | tf_op jit(solution)/shard_map/convert_element_type | solution.py:83
  253.5 41.3 %reduce-scatter.2.cloned.1.call-done = bf16[384,1024]{1,0:T(8,128)(2,1)} async-done(((bf16[1536,1024]{1,0:T(8,128)(2,1)}), bf16[384,1024]{1,0:T(8,128)(2,1)}) %reduce-scatter.2.cloned.1.call-update) | async-done | bytes 786448 | tf_op jit(solution)/shard_map/reduce_scatter | solution.py:80
  294.7 2.3 reshape.98
  297.1 10.8 %all-to-all-start.2 = ((bf16[64,6,1024]{2,1,0:T(8,128)(2,1)}), bf16[64,6,1024]{2,1,0:T(8,128)(2,1)}, u32[]{:S(2)}, u32[]{:S(2)}) async-start(bf16[64,6,1024]{2,1,0:T(8,128)(2,1)} %reshape.98), calls=%async_computation.3 | async-start | bytes 2097152 | tf_op jit(solution)/shard_map/all_to_all | solution.py:89
  309.3 26.5 %all-to-all-done.2 = bf16[64,6,1024]{2,1,0:T(8,128)(2,1)} async-done(((bf16[64,6,1024]{2,1,0:T(8,128)(2,1)}), bf16[64,6,1024]{2,1,0:T(8,128)(2,1)}, u32[]{:S(2)}, u32[]{:S(2)}) %all-to-all-start.2) | async-done | bytes 786464 | tf_op jit(solution)/shard_map/all_to_all | solution.py:89
  335.8 2.3 fusion.24
  338.1 1.8 fusion.28
  (47 shorter events, 10.7 us)
Async XLA Ops:
  6.5 1.9 copy-start
  6.5 138.0 %all-gather.4.cloned.1.call-start = ((), (), s32[]{:S(2)}) async-start(), calls=%async_computation.4 | async-start | bytes 8421376 | tf_op jit(solution)/shard_map/all_gather | solution.py:45
  13.4 5.2 %copy-start.8 = (s32[1,1,128,2]{2,3,1,0:T(2,128)S(1)}, s32[1,1,128,2]{2,3,1,0:T(2,128)}, u32[]{:S(2)}) copy-start(s32[1,1,128,2]{2,3,1,0:T(2,128)} %param.17) | copy-start | bytes 3076
  13.4 41.2 %all-to-all-start = ((bf16[2,4,128,1536]{3,2,0,1:T(8,128)(2,1)}), bf16[2,4,128,1536]{3,2,0,1:T(8,128)(2,1)S(1)}, u32[]{:S(2)}, u32[]{:S(2)}) async-start(bf16[2,4,128,1536]{3,2,0,1:T(8,128)(2,1)} %copy.26), calls=%async_computation | async-start | bytes 6291456 | tf_op jit(solution)/shard_map/all_to_all | solution.py:25
  18.6 205.6 %all-gather.6.cloned.1.call-start = ((), (), s32[]{:S(2)}) async-start(), calls=%async_computation.6 | async-start | bytes 3932160 | tf_op jit(solution)/shard_map/all_gather | solution.py:71
  56.4 5.5 %copy-start.4 = (bf16[8,128,512]{2,1,0:T(8,128)(2,1)S(1)}, bf16[8,128,512]{2,1,0:T(8,128)(2,1)}, u32[]{:S(2)}) copy-start(bf16[8,128,512]{2,1,0:T(8,128)(2,1)} %get-tuple-element.7) | copy-start | bytes 3145732
  61.8 4.4 %copy-start.3 = (bf16[8,128,512]{2,1,0:T(8,128)(2,1)S(1)}, bf16[8,128,512]{2,1,0:T(8,128)(2,1)}, u32[]{:S(2)}) copy-start(bf16[8,128,512]{2,1,0:T(8,128)(2,1)} %get-tuple-element.9) | copy-start | bytes 3145732
  66.9 3.8 %copy-start.5 = (bf16[8,128,8,64]{3,0,2,1:T(8,128)(2,1)S(1)}, bf16[8,128,8,64]{3,0,2,1:T(8,128)(2,1)}, u32[]{:S(2)}) copy-start(bf16[8,128,8,64]{3,0,2,1:T(8,128)(2,1)} %copy.30) | copy-start | bytes 3145732
  144.6 4.8 %copy-start.7 = (f32[1024]{0:T(1024)S(1)}, f32[1024]{0:T(1024)}, u32[]{:S(2)}) copy-start(f32[1024]{0:T(1024)} %param.12) | copy-start | bytes 12292
  149.3 37.1 %copy-start.2 = (f32[128,1024]{1,0:T(8,128)}, f32[128,1024]{1,0:T(8,128)S(1)}, u32[]{:S(2)}) copy-start(f32[128,1024]{1,0:T(8,128)S(1)} %get-tuple-element.13) | copy-start | bytes 1572868
  186.5 108.3 %reduce-scatter.2.cloned.1.call-start = ((), (), s32[]{:S(2)}) async-start(), calls=%async_computation.5 | async-start | bytes 3932160 | tf_op jit(solution)/shard_map/reduce_scatter | solution.py:80
  253.4 54.4 %copy-start.6 = (bf16[1024,64]{0,1:T(8,128)(2,1)S(1)}, bf16[1024,64]{0,1:T(8,128)(2,1)}, u32[]{:S(2)}) copy-start(bf16[1024,64]{0,1:T(8,128)(2,1)} %param.13) | copy-start | bytes 393220
  294.7 45.2 %copy-start.1 = (bf16[2,512,1536]{2,1,0:T(8,128)(2,1)S(1)}, bf16[2,512,1536]{2,1,0:T(8,128)(2,1)}, u32[]{:S(2)}) copy-start(bf16[2,512,1536]{2,1,0:T(8,128)(2,1)} %param.10) | copy-start | bytes 9437188
  297.1 38.7 %all-to-all-start.2 = ((bf16[64,6,1024]{2,1,0:T(8,128)(2,1)}), bf16[64,6,1024]{2,1,0:T(8,128)(2,1)}, u32[]{:S(2)}, u32[]{:S(2)}) async-start(bf16[64,6,1024]{2,1,0:T(8,128)(2,1)} %reshape.98), calls=%async_computation.3 | async-start | bytes 2097152 | tf_op jit(solution)/shard_map/all_to_all | solution.py:89
Sparse Core Ops, SparseCore 0:
  10.9 133.5 all-gather.3
  186.6 37.5 all-gather.5
  253.6 41.0 reduce-scatter.1
where the time goes:
time: 347 us; the launch traced here: 346 us
  waiting for transfers between devices  201 us (58%)
  matrix products  42.3 us (12%)
  local copies, waits for them, and re-layouts  36.6 us (11%)
  blocking collectives  35.1 us (10%)
  starting transfers between devices  16 us (5%)
  between operations  13.3 us (4%)
    all_gather x1, waiting for transfers between devices, body(): lax.all_gather(w_join, ('mic', 'seq'), axis=0, tiled=True)  59.5 us
    reduce_scatter x1, waiting for transfers between devices, body(): lax.psum_scatter(result.reshape(lax.axis_size('mic') * (seq_count * exp_l...  41.3 us
    all_gather x1, waiting for transfers between devices, body(): arrived = lax.all_gather(landed[None], 'mic', axis=0, tiled=True)  37.7 us
    all_to_all x1, waiting for transfers between devices, body(): lax.all_to_all(projected, 'mic', split_axis=1, concat_axis=0, tiled=True)  35.4 us
    all_to_all x1, blocking collectives, body(): lax.all_to_all(buffers, 'seq', split_axis=0, concat_axis=0, tiled=True)  35.1 us
    all_to_all x1, waiting for transfers between devices, body(): lax.all_to_all(summed, 'seq', split_axis=0, concat_axis=0, tiled=True)  26.5 us
    all_to_all x1, starting transfers between devices, body(): lax.all_to_all(summed, 'seq', split_axis=0, concat_axis=0, tiled=True)  10.8 us
    dot_general x1, matrix products, body(): jnp.einsum('nejf,efd->nejd', inner, w_down, preferred_element_type=jnp.fl...  10.6 us
  transfers between devices with their start and end apart: 5, of which 5 were waited for; matrix products, arithmetic and copies ran while one was open for 11% of the time, Pallas kernels for 0%

commit v1 on v0

--- a/solution.py
+++ b/solution.py
@@ -6,6 +6,27 @@
 MICS = 8
 HEADS = 8
 TOP = 2
+
+
+def gather_around(value, axis, dim):
+    size, index, width = (lax.axis_size(axis), lax.axis_index(axis), value.shape[dim])
+    upward = [(i, (i + 1) % size) for i in range(size)]
+    left = [(i, (i - 1) % size) for i in range(size)]
+    result = jnp.zeros((*value.shape[:dim], size * width, *value.shape[dim + 1 :]), value.dtype)
+    result = lax.dynamic_update_slice_in_dim(result, value, index * width, axis=dim)
+    from_left = from_right = value
+    halfway = size // 2
+    for step in range(1, halfway + 1):
+        from_left = lax.ppermute(from_left, axis, upward)
+        result = lax.dynamic_update_slice_in_dim(
+            result, from_left, (index - step) % size * width, axis=dim
+        )
+        if step < size - halfway:
+            from_right = lax.ppermute(from_right, axis, left)
+            result = lax.dynamic_update_slice_in_dim(
+                result, from_right, (index + step) % size * width, axis=dim
+            )
+    return result
 
 
 def body(frames_in, w_qkv, w_join, norm_gain, w_router, w_gate, w_up, w_down, expert_ids):
@@ -68,7 +89,7 @@
     ).astype(jnp.bfloat16)
     buffers = buffers.reshape(seq_count, exp_local * capacity, model_width)
     landed = lax.all_to_all(buffers, "seq", split_axis=0, concat_axis=0, tiled=True)
-    arrived = lax.all_gather(landed[None], "mic", axis=0, tiled=True)
+    arrived = gather_around(landed[None], "mic", 0)
     flat = arrived.reshape(mic_count * seq_count * exp_local * capacity, model_width)
     piece_rows = flat.reshape(-1, exp_local, capacity, model_width)
     first_proj = jnp.einsum(

time: 347 us -> 342 us (0.986)
  waiting for transfers between devices: 201 us -> 193 us
    all_gather x1 -> x0, waiting for transfers between devices: 37.7 us -> none  [body(): arrived = lax.all_gather(landed[None], 'mic', axis=0, tiled=True)]
    ppermute x0 -> x3, waiting for transfers between devices: none -> 32 us  [the longest x2 31.9 us: gather_around(): from_left = lax.ppermute(from_left, axis, upward)]
  transfers between devices with their start and end apart: 5 -> 7, of which waited for: 5 -> 6; matrix products, arithmetic and copies ran while one was open for 11% -> 12% of each run, Pallas kernels for 0% -> 0%
where the time goes in v1:
time: 342 us
  waiting for transfers between devices  193 us (56%)
  local copies, waits for them, and re-layouts  40 us (12%)
  matrix products  38.9 us (11%)
  blocking collectives  35.1 us (10%)
  starting transfers between devices  18.7 us (5%)
  between operations  13.6 us (4%)
    all_gather x1, waiting for transfers between devices, body(): lax.all_gather(w_join, ('mic', 'seq'), axis=0, tiled=True)  59.5 us
    reduce_scatter x1, waiting for transfers between devices, body(): lax.psum_scatter(result.reshape(lax.axis_size('mic') * (seq_count * exp_l...  39.1 us
    all_to_all x1, waiting for transfers between devices, body(): lax.all_to_all(projected, 'mic', split_axis=1, concat_axis=0, tiled=True)  35.4 us
    all_to_all x1, blocking collectives, body(): lax.all_to_all(buffers, 'seq', split_axis=0, concat_axis=0, tiled=True)  35.1 us
    ppermute x2, waiting for transfers between devices, gather_around(): from_left = lax.ppermute(from_left, axis, upward)  31.9 us
    all_to_all x1, waiting for transfers between devices, body(): lax.all_to_all(summed, 'seq', split_axis=0, concat_axis=0, tiled=True)  26.5 us
    all_to_all x1, starting transfers between devices, body(): lax.all_to_all(summed, 'seq', split_axis=0, concat_axis=0, tiled=True)  10.8 us
    dot_general x1, matrix products, body(): jnp.einsum('nejf,efd->nejd', inner, w_down, preferred_element_type=jnp.fl...  10.6 us
  transfers between devices with their start and end apart: 7, of which 6 were waited for; matrix products, arithmetic and copies ran while one was open for 12% of the time, Pallas kernels for 0%

profile of v1, /device:TPU:1, one launch (start us, length us, event | category | flops | bytes accessed | tf_op | source)
XLA Modules:
  0.0 341.7 jit_solution(9862878899361845598)
XLA Ops:
  8.4 3.0 convolution_convert_fusion
  13.4 5.1 %all-to-all-start = ((bf16[2,4,128,1536]{3,2,0,1:T(8,128)(2,1)}), bf16[2,4,128,1536]{3,2,0,1:T(8,128)(2,1)S(1)}, u32[]{:S(2)}, u32[]{:S(2)}) async-start(bf16[2,4,128,1536]{3,2,0,1:T(8,128)(2,1)} %copy.32), calls=%async_computation | async-start | bytes 6291456 | tf_op jit(solution)/shard_map/all_to_all | solution.py:46
  19.2 35.4 %all-to-all-done = bf16[2,4,128,1536]{3,2,0,1:T(8,128)(2,1)S(1)} async-done(((bf16[2,4,128,1536]{3,2,0,1:T(8,128)(2,1)}), bf16[2,4,128,1536]{3,2,0,1:T(8,128)(2,1)S(1)}, u32[]{:S(2)}, u32[]{:S(2)}) %all-to-all-start) | async-done | bytes 3145760 | tf_op jit(solution)/shard_map/all_to_all | solution.py:46
  58.1 3.8 %copy.36 = bf16[8,128,8,64]{3,0,2,1:T(8,128)(2,1)} copy(bf16[8,128,8,64]{1,3,2,0:T(8,128)(2,1)S(1)} %bitcast.113) | data formatting | bytes 2097152 | tf_op jit(solution)/shard_map/reshape | solution.py:49
  62.5 3.7 %copy.37 = bf16[8,128,8,64]{3,0,2,1:T(8,128)(2,1)} copy(bf16[8,128,8,64]{1,3,2,0:T(8,128)(2,1)S(1)} %bitcast.114) | data formatting | bytes 2097152 | tf_op jit(solution)/shard_map/reshape | solution.py:50
  66.9 3.7 %copy.38 = bf16[8,128,8,64]{3,0,2,1:T(8,128)(2,1)} copy(bf16[8,128,8,64]{1,3,2,0:T(8,128)(2,1)S(1)} %bitcast.115) | data formatting | bytes 2097152 | tf_op jit(solution)/shard_map/reshape | solution.py:53
  70.6 6.6 %fusion.38 = (f32[128,8,8]{2,1,0:T(8,128)S(1)}, f32[128,8,8,8]{2,3,1,0:T(8,128)}) fusion(bf16[8,128,8,64]{3,0,2,1:T(8,128)(2,1)S(1)} %copy-done.6, bf16[8,128,8,64]{3,0,2,1:T(8,128)(2,1)} %copy.37), kind=kOutput, calls=%fused_computation.60 | convolution fusion | flops 8585223 | bytes 2392064 | tf_op jit(solution)/shard_map/sub | solution.py:58
  77.2 4.7 %convert_bitcast_fusion.1 = bf16[128,8,8,64]{3,1,2,0:T(8,128)(2,1)} fusion(bf16[8,128,8,64]{3,0,2,1:T(8,128)(2,1)} %copy.38, f32[128,8,8,8]{2,3,1,0:T(8,128)} %get-tuple-element.11, f32[128,8,8]{2,1,0:T(8,128)S(1)} %get-tuple-element.10), kind=kOutput, calls=%fused_computation.22 | convolution fusion | flops 9043968 | bytes 2392064 | tf_op jit(solution)/shard_map/fhij,jfhd->fihd/dot_general | solution.py:60
  81.9 3.2 copy.40
  85.1 59.5 %all-gather.2.cloned.1.call-done = bf16[4096,1024]{1,0:T(8,128)(2,1)} async-done(((bf16[16,1024]{1,0:T(8,128)(2,1)}), bf16[4096,1024]{1,0:T(8,128)(2,1)}) %all-gather.2.cloned.1.call-update) | async-done | bytes 8388624 | tf_op jit(solution)/shard_map/all_gather | solution.py:66
  144.6 4.7 %multiply_reduce_fusion.1 = (f32[128]{0:T(128)S(1)}, f32[128,1024]{1,0:T(8,128)S(1)}) fusion(bf16[128,4096]{0,1:T(8,128)(2,1)S(1)} %bitcast.112, bf16[4096,1024]{1,0:T(8,128)(2,1)} %all-gather.2.cloned.1.call-done), kind=kOutput, calls=%fused_computation.37 | convolution fusion | flops 1074003840 | bytes 9961984 | tf_op jit(solution)/shard_map/dot_general | solution.py:64
  150.4 35.1 %all_to_all.25 = bf16[64,6,1024]{2,1,0:T(8,128)(2,1)S(1)} all-to-all(bf16[64,6,1024]{2,1,0:T(8,128)(2,1)S(1)} %reshape.92), channel_id=1, replica_groups=mesh['mic'=4,'seq'=64] {'seq'}, dimensions={0} | all-to-all | bytes 1572864 | tf_op jit(solution)/shard_map/all_to_all | solution.py:91
  186.0 2.7 collective-permute-start.1
  188.6 16.2 %collective-permute-done = bf16[1,64,6,1024]{3,1,2,0:T(8,128)(2,1)S(1)} collective-permute-done((bf16[1,64,6,1024]{3,1,2,0:T(8,128)(2,1)S(1)}, bf16[1,64,6,1024]{3,1,2,0:T(8,128)(2,1)S(1)}, u32[]{:S(2)}, u32[]{:S(2)}) %collective-permute-start) | collective-permute-done | bytes 786464 | tf_op jit(solution)/shard_map/ppermute | solution.py:20
  207.1 15.7 %collective-permute-done.2 = bf16[1,64,6,1024]{3,1,2,0:T(8,128)(2,1)S(1)} collective-permute-done((bf16[1,64,6,1024]{3,1,2,0:T(8,128)(2,1)S(1)}, bf16[1,64,6,1024]{3,1,2,0:T(8,128)(2,1)S(1)}, u32[]{:S(2)}, u32[]{:S(2)}) %collective-permute-start.2) | collective-permute-done | bytes 786464 | tf_op jit(solution)/shard_map/ppermute | solution.py:20
  224.6 5.3 %fusion.19 = f32[256,6,1024]{2,0,1:T(8,128)} fusion(bf16[256,6,1024]{2,0,1:T(8,128)(2,1)S(1)} %bitcast.117, bf16[1,1024,1024]{2,1,0:T(8,128)(2,1)S(1)} %copy-done.10), kind=kOutput, calls=%fused_computation.20 | convolution fusion | flops 3221225472 | bytes 11534336 | tf_op jit(solution)/shard_map/nejd,edf->nejf/dot_general | solution.py:95
  229.9 10.6 %convert_bitcast_fusion = bf16[256,1,6,1024]{3,0,2,1:T(8,128)(2,1)S(1)} fusion(f32[256,6,1024]{2,0,1:T(8,128)} %fusion.19, bf16[256,6,1024]{2,0,1:T(8,128)(2,1)} %bitcast.118, bf16[1,1024,1024]{2,1,0:T(8,128)(2,1)} %param.16, bf16[1,1024,1024]{2,1,0:T(8,128)(2,1)} %param.15), kind=kOutput, calls=%fused_computation.15 | convolution fusion | flops 6453460992 | bytes 16777216 | tf_op jit(solution)/shard_map/nejf,efd->nejd/dot_general | solution.py:100
  240.4 3.7 %copy.51 = bf16[256,1,6,1024]{3,2,0,1:T(8,128)(2,1)} copy(bf16[256,1,6,1024]{3,0,2,1:T(8,128)(2,1)S(1)} %convert_bitcast_fusion) | data formatting | bytes 6291456 | tf_op jit(solution)/shard_map/convert_element_type | solution.py:104
  244.2 6.3 %convert_element_type.71 = bf16[1536,1024]{1,0:T(8,128)(2,1)} reshape(bf16[256,1,6,1024]{3,2,0,1:T(8,128)(2,1)} %copy.51) | data formatting | bytes 6291456 | tf_op jit(solution)/shard_map/convert_element_type | solution.py:104
  250.5 39.1 %reduce-scatter.2.cloned.1.call-done = bf16[384,1024]{1,0:T(8,128)(2,1)} async-done(((bf16[1536,1024]{1,0:T(8,128)(2,1)}), bf16[384,1024]{1,0:T(8,128)(2,1)}) %reduce-scatter.2.cloned.1.call-update) | async-done | bytes 786448 | tf_op jit(solution)/shard_map/reduce_scatter | solution.py:101
  289.7 2.3 reshape.98
  292.0 10.8 %all-to-all-start.2 = ((bf16[64,6,1024]{2,1,0:T(8,128)(2,1)}), bf16[64,6,1024]{2,1,0:T(8,128)(2,1)}, u32[]{:S(2)}, u32[]{:S(2)}) async-start(bf16[64,6,1024]{2,1,0:T(8,128)(2,1)} %reshape.98), calls=%async_computation.3 | async-start | bytes 2097152 | tf_op jit(solution)/shard_map/all_to_all | solution.py:110
  304.2 26.5 %all-to-all-done.2 = bf16[64,6,1024]{2,1,0:T(8,128)(2,1)} async-done(((bf16[64,6,1024]{2,1,0:T(8,128)(2,1)}), bf16[64,6,1024]{2,1,0:T(8,128)(2,1)}, u32[]{:S(2)}, u32[]{:S(2)}) %all-to-all-start.2) | async-done | bytes 786464 | tf_op jit(solution)/shard_map/all_to_all | solution.py:110
  330.7 2.3 fusion.24
  (59 shorter events, 17.9 us)
Async XLA Ops:
  6.5 1.9 copy-start
  6.5 138.0 %all-gather.2.cloned.1.call-start = ((), (), s32[]{:S(2)}) async-start(), calls=%async_computation.4 | async-start | bytes 8421376 | tf_op jit(solution)/shard_map/all_gather | solution.py:66
  13.4 5.2 %copy-start.9 = (s32[1,1,128,2]{2,3,1,0:T(2,128)S(1)}, s32[1,1,128,2]{2,3,1,0:T(2,128)}, u32[]{:S(2)}) copy-start(s32[1,1,128,2]{2,3,1,0:T(2,128)} %param.17) | copy-start | bytes 3076
  13.4 41.2 %all-to-all-start = ((bf16[2,4,128,1536]{3,2,0,1:T(8,128)(2,1)}), bf16[2,4,128,1536]{3,2,0,1:T(8,128)(2,1)S(1)}, u32[]{:S(2)}, u32[]{:S(2)}) async-start(bf16[2,4,128,1536]{3,2,0,1:T(8,128)(2,1)} %copy.32), calls=%async_computation | async-start | bytes 6291456 | tf_op jit(solution)/shard_map/all_to_all | solution.py:46
  18.6 271.1 %reduce-scatter.2.cloned.1.call-start = ((), (), s32[]{:S(2)}) async-start(), calls=%async_computation.5 | async-start | bytes 3932160 | tf_op jit(solution)/shard_map/reduce_scatter | solution.py:101
  56.4 5.5 %copy-start.4 = (bf16[8,128,512]{2,1,0:T(8,128)(2,1)S(1)}, bf16[8,128,512]{2,1,0:T(8,128)(2,1)}, u32[]{:S(2)}) copy-start(bf16[8,128,512]{2,1,0:T(8,128)(2,1)} %get-tuple-element.7) | copy-start | bytes 3145732
  61.8 4.4 %copy-start.3 = (bf16[8,128,512]{2,1,0:T(8,128)(2,1)S(1)}, bf16[8,128,512]{2,1,0:T(8,128)(2,1)}, u32[]{:S(2)}) copy-start(bf16[8,128,512]{2,1,0:T(8,128)(2,1)} %get-tuple-element.9) | copy-start | bytes 3145732
  66.9 3.8 %copy-start.6 = (bf16[8,128,8,64]{3,0,2,1:T(8,128)(2,1)S(1)}, bf16[8,128,8,64]{3,0,2,1:T(8,128)(2,1)}, u32[]{:S(2)}) copy-start(bf16[8,128,8,64]{3,0,2,1:T(8,128)(2,1)} %copy.36) | copy-start | bytes 3145732
  144.6 4.8 %copy-start.8 = (f32[1024]{0:T(1024)S(1)}, f32[1024]{0:T(1024)}, u32[]{:S(2)}) copy-start(f32[1024]{0:T(1024)} %param.12) | copy-start | bytes 12292
  149.3 0.8 copy-start.2
  185.9 19.0 %collective-permute-start = (bf16[1,64,6,1024]{3,1,2,0:T(8,128)(2,1)S(1)}, bf16[1,64,6,1024]{3,1,2,0:T(8,128)(2,1)S(1)}, u32[]{:S(2)}, u32[]{:S(2)}) collective-permute-start(bf16[1,64,6,1024]{3,1,2,0:T(8,128)(2,1)S(1)} %copy.46), channel_id=1, source_target_pairs={{0,64},{64,128},{128,192},{192,0},{1,65},{65,129},{129,193},{193,1... | collective-permute-start | bytes 2359304 | tf_op jit(solution)/shard_map/ppermute | solution.py:20
  186.0 19.8 %collective-permute-start.1 = (bf16[1,64,6,1024]{3,1,2,0:T(8,128)(2,1)S(1)}, bf16[1,64,6,1024]{3,1,2,0:T(8,128)(2,1)}, u32[]{:S(2)}, u32[]{:S(2)}) collective-permute-start(bf16[1,64,6,1024]{3,1,2,0:T(8,128)(2,1)S(1)} %copy.46), channel_id=1, source_target_pairs={{0,192},{64,0},{128,64},{192,128},{1,193},{65,1},{129,65},{193,129... | collective-permute-start | bytes 2359304 | tf_op jit(solution)/shard_map/ppermute | solution.py:25
  204.9 18.0 %collective-permute-start.2 = (bf16[1,64,6,1024]{3,1,2,0:T(8,128)(2,1)S(1)}, bf16[1,64,6,1024]{3,1,2,0:T(8,128)(2,1)S(1)}, u32[]{:S(2)}, u32[]{:S(2)}) collective-permute-start(bf16[1,64,6,1024]{3,1,2,0:T(8,128)(2,1)S(1)} %collective-permute-done), channel_id=1, source_target_pairs={{0,64},{64,128},{128,192},{192,0},{1,65},{65,129},{129,193},{193,1... | collective-permute-start | bytes 2359304 | tf_op jit(solution)/shard_map/ppermute | solution.py:20
  205.2 19.3 %copy-start.10 = (bf16[1,1024,1024]{2,1,0:T(8,128)(2,1)S(1)}, bf16[1,1024,1024]{2,1,0:T(8,128)(2,1)}, u32[]{:S(2)}) copy-start(bf16[1,1024,1024]{2,1,0:T(8,128)(2,1)} %param.14) | copy-start | bytes 6291460
  222.9 1.7 copy-start.5
  250.5 52.3 %copy-start.7 = (bf16[1024,64]{0,1:T(8,128)(2,1)S(1)}, bf16[1024,64]{0,1:T(8,128)(2,1)}, u32[]{:S(2)}) copy-start(bf16[1024,64]{0,1:T(8,128)(2,1)} %param.13) | copy-start | bytes 393220
  289.7 45.2 %copy-start.1 = (bf16[2,512,1536]{2,1,0:T(8,128)(2,1)S(1)}, bf16[2,512,1536]{2,1,0:T(8,128)(2,1)}, u32[]{:S(2)}) copy-start(bf16[2,512,1536]{2,1,0:T(8,128)(2,1)} %param.10) | copy-start | bytes 9437188
  292.0 38.7 %all-to-all-start.2 = ((bf16[64,6,1024]{2,1,0:T(8,128)(2,1)}), bf16[64,6,1024]{2,1,0:T(8,128)(2,1)}, u32[]{:S(2)}, u32[]{:S(2)}) async-start(bf16[64,6,1024]{2,1,0:T(8,128)(2,1)} %reshape.98), calls=%async_computation.3 | async-start | bytes 2097152 | tf_op jit(solution)/shard_map/all_to_all | solution.py:110
Sparse Core Ops, SparseCore 0:
  10.9 133.5 all-gather.1
  250.7 38.9 reduce-scatter.1
